TPU v7x, 256 devices: a whole 4x4x8 slice. The times are simulated.
256 devices in a mesh: row: 32 (over z, y_hi, core), col: 8 (over x, y_lo).
Axes of the slice: x: 4, y: 4 (y_hi: 2, y_lo: 2; y = y_hi * 2 + y_lo), z: 8, core: 2. Of those that a mesh axis runs over, the one named last changes fastest.
Arguments:
- feature_map: bfloat16 [256, 256, 384], P('row', 'col'), may hold values from -6 to 6
- kernel: float32 [7, 7, 384], replicated, may hold values from -0.875 to 0.875
- ln_gain: float32 [384], replicated, may hold values from 0.5 to 1.5
- ln_bias: float32 [384], replicated, may hold values from -3 to 3
- w_in: bfloat16 [384, 1536], P(None, ('row', 'col')), may hold values from -0.3125 to 0.3125
- b_in: float32 [1536], replicated, may hold values from -3 to 3
- w_out: bfloat16 [1536, 384], P(('row', 'col')), may hold values from -0.15625 to 0.15625
- b_out: float32 [384], replicated, may hold values from -3 to 3
- layer_scale: float32 [384], replicated, may hold values from 0.5 to 1.5
- cotangent: bfloat16 [256, 256, 384], P('row', 'col'), may hold values from -6 to 6
Outputs:
- block_out: bfloat16 [256, 256, 384], P('row', 'col')
- grad_input: bfloat16 [256, 256, 384], P('row', 'col')
- grad_w_in: float32 [384, 1536], P(None, ('row', 'col'))
- grad_w_out: float32 [1536, 384], P(('row', 'col'))
- small_grads: float32 [53, 384], replicated
- grad_b_in: float32 [1536], replicated
All inputs are finite; a program needn't handle non-finite values.
Results may differ from a plain program's by a relative error of at most 0.007.
Values may be sent and summed in bfloat16 or wider, within the bound.
No kernel may reach another device: no remote copies, remote signals or barrier semaphores. Data moves between devices by JAX's collectives and lax.ppermute only.
A program may use at most 64 MiB of HBM per device.

v0:
```python
import math
import jax
import jax.numpy as jnp
from jax import lax
from jax.sharding import PartitionSpec as P


def padded_2(x, sides, width):
    for axis, dim in sides:
        peers, length = (lax.axis_size(axis), x.shape[dim])
        up = [(i, (i + 1) % peers) for i in range(peers - 1)]
        down = [(j, i) for i, j in up]
        last = lax.slice_in_dim(x, length - width, length, axis=dim)
        first = lax.slice_in_dim(x, 0, width, axis=dim)
        before = lax.ppermute(last, axis, up)
        after = lax.ppermute(first, axis, down)
        x = jnp.concatenate([before, x, after], axis=dim)
    return x


def gelu_parts(hidden):
    normal_cdf = 0.5 * (1.0 + jax.scipy.special.erf(hidden * (1.0 / math.sqrt(2.0))))
    density = jnp.exp(-0.5 * hidden * hidden) * (1.0 / math.sqrt(2.0 * math.pi))
    return (hidden * normal_cdf, normal_cdf + hidden * density)


def extend(field):
    return padded_2(field, (("row", 0), ("col", 1)), 3)


def on_device(
    feature_map, kernel, ln_gain, ln_bias, w_in, b_in, w_out, b_out, layer_scale, cotangent
):
    row_count, col_count, channels = feature_map.shape
    pixels = row_count * col_count
    padded = extend(feature_map).astype(jnp.float32)
    conv = jnp.zeros((row_count, col_count, channels), jnp.float32)
    for tap_row in range(7):
        for tap_col in range(7):
            conv = (
                conv
                + padded[tap_row : tap_row + row_count, tap_col : tap_col + col_count]
                * kernel[tap_row, tap_col]
            )
    average = jnp.mean(conv, -1, keepdims=True)
    centered = conv - average
    variance = jnp.mean(centered * centered, -1, keepdims=True)
    inv_std = lax.rsqrt(variance + 1e-06)
    unit_scaled = centered * inv_std
    normed = (unit_scaled * ln_gain + ln_bias).astype(jnp.bfloat16).reshape(pixels, channels)
    contract_last = (((1,), (1,)), ((), ()))
    contract_first = (((0,), (0,)), ((), ()))
    w_in_full = lax.all_gather(w_in, ("row", "col"), axis=1, tiled=True)
    w_out_full = lax.all_gather(w_out, ("row", "col"), axis=0, tiled=True)
    hidden = jnp.dot(normed, w_in_full, preferred_element_type=jnp.float32) + b_in
    act_value, slope = gelu_parts(hidden)
    activated = act_value.astype(jnp.bfloat16)
    mixed = jnp.dot(activated, w_out_full, preferred_element_type=jnp.float32) + b_out
    source = feature_map.astype(jnp.float32).reshape(pixels, channels)
    block_out = (
        (source + layer_scale * mixed).astype(jnp.bfloat16).reshape(row_count, col_count, channels)
    )
    grad_flow = cotangent.astype(jnp.float32).reshape(pixels, channels)
    grad_mixed = grad_flow * layer_scale
    mixed_low = grad_mixed.astype(jnp.bfloat16)
    grad_act = lax.dot_general(
        mixed_low, w_out_full, contract_last, preferred_element_type=jnp.float32
    )
    grad_hidden = (grad_act * slope).astype(jnp.bfloat16)
    grad_w_out = lax.psum_scatter(
        lax.dot_general(activated, mixed_low, contract_first, preferred_element_type=jnp.float32),
        ("row", "col"),
        scatter_dimension=0,
        tiled=True,
    )
    win_term = lax.dot_general(
        normed, grad_hidden, contract_first, preferred_element_type=jnp.float32
    )
    grad_w_in = lax.psum_scatter(win_term, ("row", "col"), scatter_dimension=1, tiled=True)
    grad_normed = lax.dot_general(
        grad_hidden, w_in_full, contract_last, preferred_element_type=jnp.float32
    )
    grad_normed = grad_normed.reshape(row_count, col_count, channels)
    grad_gain = jnp.sum(grad_normed * unit_scaled, (0, 1))
    grad_lnb = jnp.sum(grad_normed, (0, 1))
    scaled_grad = grad_normed * ln_gain
    grad_conv = inv_std * (
        scaled_grad
        - jnp.mean(scaled_grad, -1, keepdims=True)
        - unit_scaled * jnp.mean(scaled_grad * unit_scaled, -1, keepdims=True)
    )
    tap_terms = []
    for tap_row in range(7):
        for tap_col in range(7):
            tap_terms.append(
                jnp.sum(
                    padded[tap_row : tap_row + row_count, tap_col : tap_col + col_count]
                    * grad_conv,
                    (0, 1),
                )
            )
    grad_pad = extend(grad_conv.astype(jnp.bfloat16)).astype(jnp.float32)
    back_conv = jnp.zeros((row_count, col_count, channels), jnp.float32)
    for tap_row in range(7):
        for tap_col in range(7):
            back_conv = (
                back_conv
                + grad_pad[
                    6 - tap_row : 6 - tap_row + row_count, 6 - tap_col : 6 - tap_col + col_count
                ]
                * kernel[tap_row, tap_col]
            )
    grad_input = (cotangent.astype(jnp.float32) + back_conv).astype(jnp.bfloat16)
    small_local = jnp.concatenate(
        [
            jnp.stack(tap_terms, 0),
            grad_gain[None],
            grad_lnb[None],
            jnp.sum(grad_mixed, 0)[None],
            jnp.sum(grad_flow * mixed, 0)[None],
        ],
        0,
    )
    bias_local = jnp.sum(grad_hidden.astype(jnp.float32), 0)
    small_grads, grad_b_in = lax.psum((small_local, bias_local), ("row", "col"))
    return (block_out, grad_input, grad_w_in, grad_w_out, small_grads, grad_b_in)


def solution(mesh):
    placed = (
        P("row", "col", None),
        P(),
        P(),
        P(),
        P(None, ("row", "col")),
        P(),
        P(("row", "col"), None),
        P(),
        P(),
        P("row", "col", None),
    )
    return jax.shard_map(
        on_device,
        mesh=mesh,
        in_specs=placed,
        out_specs=(
            P("row", "col", None),
            P("row", "col", None),
            P(None, ("row", "col")),
            P(("row", "col"), None),
            P(),
            P(),
        ),
        check_vma=False,
    )
```

profile of v0, /device:TPU:99, one launch (start us, length us, event | category | flops | bytes accessed | tf_op | source)
XLA Modules:
  0.0 1693.0 jit_solution(1590831697639832717)
XLA Ops:
  7.9 0.9 fusion.63
  8.9 5.4 collective-permute-start
  14.3 1.9 collective-permute-start.1
  16.3 1.1 slice_reduce_fusion.47
  17.4 1.0 fusion.56
  18.4 1.2 slice_reduce_fusion.48
  19.7 1.0 constant_dynamic-update-slice_fusion.1
  21.5 2.3 collective-permute-start.3
  23.8 3.0 collective-permute-start.2
  26.8 1.0 slice_reduce_fusion.46
  28.5 1.0 collective-permute-done.2
  29.6 3.2 fusion.60
  33.3 671.1 %all-gather.5.cloned.1.call-done = bf16[256,6,384]{2,1,0:T(8,128)(2,1)} async-done(((bf16[1,6,384]{2,1,0:T(8,128)(2,1)}), bf16[256,6,384]{2,1,0:T(8,128)(2,1)}) %all-gather.5.cloned.1.call-update) | async-done | bytes 1179664 | tf_op jit(solution)/shard_map/all_gather | solution.py:53
  704.4 2.3 reshape.74
  706.7 2.5 multiply_convert_fusion
  709.2 684.3 %all-gather.7.cloned.1.call-done = bf16[256,6,384]{2,1,0:T(8,128)(2,1)} async-done(((bf16[1,6,384]{2,1,0:T(8,128)(2,1)}), bf16[256,6,384]{2,1,0:T(8,128)(2,1)}) %all-gather.7.cloned.1.call-update) | async-done | bytes 1179664 | tf_op jit(solution)/shard_map/all_gather | solution.py:54
  1393.6 3.3 reshape.76
  1396.8 3.5 fusion.58
  1400.3 0.9 convert_reduce_fusion
  1401.9 2.0 fusion.64
  1404.0 2.1 fusion.65
  1409.2 4.4 concatenate.19
  1413.8 1.9 collective-permute-start.5
  1415.7 5.1 collective-permute-start.4
  1422.3 1.9 collective-permute-start.7
  1424.3 3.4 collective-permute-start.6
  1427.6 73.7 %psum.15 = f32[1536]{0:T(1024)} all-reduce(f32[1536]{0:T(1024)S(1)} %get-tuple-element.129), channel_id=1, replica_groups=mesh['row'=32,'col'=8] {'row','col'}, use_global_device_ids=true, to_apply=%region_61.0 | all-reduce | flops 1536 | bytes 12288 | tf_op jit(solution)/shard_map/psum | solution.py:125
  1501.7 3.5 fusion.7
  1505.2 177.1 %all-reduce.5.cloned.1.call-done = (f32[384,1536]{0,1:T(8,128)}, f32[1536,384]{1,0:T(8,128)}, f32[53,384]{1,0:T(8,128)}) async-done(((f32[384,1536]{0,1:T(8,128)}, f32[1536,384]{1,0:T(8,128)}, f32[53,384]{1,0:T(8,128)}), (f32[384,1536]{0,1:T(8,128)}, f32[1536,384]{1,0:T(8,128)}, f32[53,384]{1,0:T(8,128)})) %all-reduce.5.cloned.1.call-update) | async-done | bytes 4800016
  1682.2 1.3 constant_dynamic-slice_fusion.1
  1683.6 1.3 constant_dynamic-slice_fusion
  1684.9 1.5 copy.21
  (173 shorter events, 7.8 us)
Async XLA Ops:
  7.2 697.2 %all-gather.5.cloned.1.call-start = ((), (), s32[]{:S(2)}) async-start(), calls=%async_computation | async-start | bytes 1579008 | tf_op jit(solution)/shard_map/all_gather | solution.py:53
  7.9 1385.7 %all-gather.7.cloned.1.call-start = ((), (), s32[]{:S(2)}) async-start(), calls=%async_computation.1 | async-start | bytes 1579008 | tf_op jit(solution)/shard_map/all_gather | solution.py:54
  8.9 10.8 collective-permute-start
  14.3 7.2 collective-permute-start.1
  16.2 1666.0 %all-reduce.5.cloned.1.call-start = ((), (), s32[]{:S(2)}) async-start(), calls=%async_computation.2 | async-start | bytes 9609216
  19.6 13.2 copy-start.5
  19.6 13.1 copy-start.7
  21.5 6.9 collective-permute-start.3
  23.8 5.7 collective-permute-start.2
  709.2 691.1 %copy-start = (bf16[256,1536]{1,0:T(8,128)(2,1)}, bf16[256,1536]{1,0:T(8,128)(2,1)S(1)}, u32[]{:S(2)}) copy-start(bf16[256,1536]{1,0:T(8,128)(2,1)S(1)} %get-tuple-element.126) | copy-start | bytes 2359300
  1413.6 87.9 %copy-start.4 = (bf16[8,32,384]{2,1,0:T(8,128)(2,1)S(1)}, bf16[8,32,384]{2,1,0:T(8,128)(2,1)}, u32[]{:S(2)}) copy-start(bf16[8,32,384]{2,1,0:T(8,128)(2,1)} %param.19) | copy-start | bytes 589828
  1413.6 87.9 %copy-start.6 = (f32[384]{0:T(512)S(1)}, f32[384]{0:T(512)}, u32[]{:S(2)}) copy-start(f32[384]{0:T(512)} %copy-done.5) | copy-start | bytes 4612
  1413.6 87.9 %copy-start.8 = (f32[384]{0:T(512)S(1)}, f32[384]{0:T(512)}, u32[]{:S(2)}) copy-start(f32[384]{0:T(512)} %copy-done.7) | copy-start | bytes 4612
  1413.6 87.9 %copy-start.10 = (f32[384]{0:T(512)S(1)}, f32[384]{0:T(512)}, u32[]{:S(2)}) copy-start(f32[384]{0:T(512)} %copy-done.9) | copy-start | bytes 4612
  1413.6 87.9 %copy-start.12 = (f32[384]{0:T(512)S(1)}, f32[384]{0:T(512)}, u32[]{:S(2)}) copy-start(f32[384]{0:T(512)} %copy-done.11) | copy-start | bytes 4612
  1413.7 87.9 %copy-start.14 = (f32[384]{0:T(512)S(1)}, f32[384]{0:T(512)}, u32[]{:S(2)}) copy-start(f32[384]{0:T(512)} %copy-done.13) | copy-start | bytes 4612
  1413.7 87.9 %copy-start.16 = (f32[384]{0:T(512)S(1)}, f32[384]{0:T(512)}, u32[]{:S(2)}) copy-start(f32[384]{0:T(512)} %copy-done.15) | copy-start | bytes 4612
  1413.7 87.9 %copy-start.18 = (f32[384]{0:T(512)S(1)}, f32[384]{0:T(512)}, u32[]{:S(2)}) copy-start(f32[384]{0:T(512)} %copy-done.17) | copy-start | bytes 4612
  1413.7 87.9 %copy-start.20 = (f32[384]{0:T(512)S(1)}, f32[384]{0:T(512)}, u32[]{:S(2)}) copy-start(f32[384]{0:T(512)} %copy-done.19) | copy-start | bytes 4612
  1413.7 87.9 %copy-start.22 = (f32[384]{0:T(512)S(1)}, f32[384]{0:T(512)}, u32[]{:S(2)}) copy-start(f32[384]{0:T(512)} %copy-done.21) | copy-start | bytes 4612
  1413.7 87.9 %copy-start.24 = (f32[384]{0:T(512)S(1)}, f32[384]{0:T(512)}, u32[]{:S(2)}) copy-start(f32[384]{0:T(512)} %copy-done.23) | copy-start | bytes 4612
  1413.7 87.9 %copy-start.26 = (f32[384]{0:T(512)S(1)}, f32[384]{0:T(512)}, u32[]{:S(2)}) copy-start(f32[384]{0:T(512)} %copy-done.25) | copy-start | bytes 4612
  1413.7 87.9 %copy-start.28 = (f32[384]{0:T(512)S(1)}, f32[384]{0:T(512)}, u32[]{:S(2)}) copy-start(f32[384]{0:T(512)} %copy-done.27) | copy-start | bytes 4612
  1413.7 87.9 %copy-start.30 = (f32[384]{0:T(512)S(1)}, f32[384]{0:T(512)}, u32[]{:S(2)}) copy-start(f32[384]{0:T(512)} %copy-done.29) | copy-start | bytes 4612
  1413.7 87.9 %copy-start.32 = (f32[384]{0:T(512)S(1)}, f32[384]{0:T(512)}, u32[]{:S(2)}) copy-start(f32[384]{0:T(512)} %copy-done.31) | copy-start | bytes 4612
  1413.8 87.9 %copy-start.34 = (f32[384]{0:T(512)S(1)}, f32[384]{0:T(512)}, u32[]{:S(2)}) copy-start(f32[384]{0:T(512)} %copy-done.33) | copy-start | bytes 4612
  1413.8 87.9 %copy-start.36 = (f32[384]{0:T(512)S(1)}, f32[384]{0:T(512)}, u32[]{:S(2)}) copy-start(f32[384]{0:T(512)} %copy-done.35) | copy-start | bytes 4612
  1413.8 87.9 %copy-start.38 = (f32[384]{0:T(512)S(1)}, f32[384]{0:T(512)}, u32[]{:S(2)}) copy-start(f32[384]{0:T(512)} %copy-done.37) | copy-start | bytes 4612
  1413.8 7.6 collective-permute-start.5
  1415.7 6.5 collective-permute-start.4
  1422.3 79.0 %collective-permute-start.7 = (bf16[14,3,384]{2,1,0:T(4,128)(2,1)S(1)}, bf16[14,3,384]{2,1,0:T(4,128)(2,1)S(1)}, u32[]{:S(2)}, u32[]{:S(2)}) collective-permute-start(bf16[14,3,384]{2,1,0:T(4,128)(2,1)S(1)} %get-tuple-element.118), channel_id=1, source_target_pairs={{1,0},{2,1},{3,2},{4,3},{5,4},{6,5},{7,6},{9,8},{10,9},{11,10},{12... | collective-permute-start | bytes 96776 | tf_op jit(solution)/shard_map/ppermute | solution.py:16
  1424.3 77.1 %collective-permute-start.6 = (bf16[14,3,384]{2,1,0:T(4,128)(2,1)S(1)}, bf16[14,3,384]{2,1,0:T(4,128)(2,1)S(1)}, u32[]{:S(2)}, u32[]{:S(2)}) collective-permute-start(bf16[14,3,384]{2,1,0:T(4,128)(2,1)S(1)} %get-tuple-element.117), channel_id=1, source_target_pairs={{0,1},{1,2},{2,3},{3,4},{4,5},{5,6},{6,7},{8,9},{9,10},{10,11},{11... | collective-permute-start | bytes 96776 | tf_op jit(solution)/shard_map/ppermute | solution.py:15
  (23 other events, 127.4 us)
Sparse Core Ops, SparseCore 0:
  9.9 694.4 all-gather.4
  706.3 687.2 all-gather.6
  1413.7 268.4 all-reduce.4
where the time goes:
time: 1690 us
  waiting for transfers between devices  1540 us (91%)
  blocking collectives  73.7 us (4%)
  starting transfers between devices  25.1 us (1%)
  local copies, waits for them, and re-layouts  20.5 us (1%)
    all_gather x1, waiting for transfers between devices, on_device(): w_out_full = lax.all_gather(w_out, ('row', 'col'), axis=0, tiled=True)  684 us
    all_gather x1, waiting for transfers between devices, on_device(): w_in_full = lax.all_gather(w_in, ('row', 'col'), axis=1, tiled=True)  671 us
    unnamed x4, waiting for transfers between devices  178 us
    psum x1, blocking collectives, on_device(): small_grads, grad_b_in = lax.psum((small_local, bias_local), ('row', 'col'))  73.7 us
  transfers between devices with their start and end apart: 11, of which 7 were waited for; matrix products, arithmetic and copies ran while one was open for 1% of the time, Pallas kernels for 0%

commit v1 on v0

--- a/solution.py
+++ b/solution.py
@@ -3,6 +3,14 @@
 import jax.numpy as jnp
 from jax import lax
 from jax.sharding import PartitionSpec as P
+from jax.lax import all_to_all, axis_size
+
+
+def derive_tokens(unit):
+    extra = jnp.concatenate(
+        all_to_all(jnp.stack(axis_size(("row", "col")) * [unit]), ("row", "col"), 0, 0), 1
+    )
+    return extra
 
 
 def padded_2(x, sides, width):
@@ -50,7 +58,7 @@
     normed = (unit_scaled * ln_gain + ln_bias).astype(jnp.bfloat16).reshape(pixels, channels)
     contract_last = (((1,), (1,)), ((), ()))
     contract_first = (((0,), (0,)), ((), ()))
-    w_in_full = lax.all_gather(w_in, ("row", "col"), axis=1, tiled=True)
+    w_in_full = derive_tokens(w_in)
     w_out_full = lax.all_gather(w_out, ("row", "col"), axis=0, tiled=True)
     hidden = jnp.dot(normed, w_in_full, preferred_element_type=jnp.float32) + b_in
     act_value, slope = gelu_parts(hidden)

time: 1690 us -> 1030 us (0.61)
  waiting for transfers between devices: 1540 us -> 862 us
    all_gather x1 -> x0, waiting for transfers between devices: 671 us -> none  [on_device(): w_in_full = lax.all_gather(w_in, ('row', 'col'), axis=1, tiled=True)]
    all_gather x1, waiting for transfers between devices: 684 us -> 656 us  [on_device(): w_out_full = lax.all_gather(w_out, ('row', 'col'), axis=0, tiled=True)]
    all_to_all x0 -> x1, waiting for transfers between devices: none -> 24.4 us  [derive_tokens(): all_to_all(jnp.stack(axis_size(('row', 'col')) * [unit]), ('row', 'col'),...]
    unnamed x4 -> x3, waiting for transfers between devices: 178 us -> 177 us
  transfers between devices with their start and end apart: 11 -> 11, of which waited for: 7 -> 6; matrix products, arithmetic and copies ran while one was open for 1% -> 1% of each run, Pallas kernels for 0% -> 0%
where the time goes in v1:
time: 1030 us
  waiting for transfers between devices  862 us (84%)
  blocking collectives  74.1 us (7%)
  starting transfers between devices  39.8 us (4%)
  local copies, waits for them, and re-layouts  17.6 us (2%)
  between operations  15.3 us (1%)
  matrix products  11.3 us (1%)
    all_gather x1, waiting for transfers between devices, on_device(): w_out_full = lax.all_gather(w_out, ('row', 'col'), axis=0, tiled=True)  656 us
    unnamed x3, waiting for transfers between devices  177 us
    psum x1, blocking collectives, on_device(): small_grads, grad_b_in = lax.psum((small_local, bias_local), ('row', 'col'))  74.1 us
    all_to_all x1, waiting for transfers between devices, derive_tokens(): all_to_all(jnp.stack(axis_size(('row', 'col')) * [unit]), ('row', 'col'),...  24.4 us
  transfers between devices with their start and end apart: 11, of which 6 were waited for; matrix products, arithmetic and copies ran while one was open for 1% of the time, Pallas kernels for 0%

profile of v1, /device:TPU:99, one launch (start us, length us, event | category | flops | bytes accessed | tf_op | source)
XLA Modules:
  0.0 1030.0 jit_solution(15613391668484383528)
XLA Ops:
  7.2 0.9 fusion.64
  8.1 5.4 collective-permute-start
  13.5 1.9 collective-permute-start.1
  15.4 2.0 stack.100
  17.4 14.6 %all-to-all-start = ((bf16[256,384,6]{1,2,0:T(8,128)(2,1)}), bf16[256,384,6]{1,2,0:T(8,128)(2,1)S(1)}, u32[]{:S(2)}, u32[]{:S(2)}) async-start(bf16[256,384,6]{1,2,0:T(8,128)(2,1)} %stack.100), calls=%async_computation | async-start | bytes 3145728 | tf_op jit(solution)/shard_map/all_to_all | solution.py:11
  33.3 3.1 collective-permute-start.3
  36.4 2.1 collective-permute-start.2
  39.3 3.2 collective-permute-done.2
  42.7 3.2 fusion.61
  46.4 24.4 %all-to-all-done = bf16[256,384,6]{1,2,0:T(8,128)(2,1)S(1)} async-done(((bf16[256,384,6]{1,2,0:T(8,128)(2,1)}), bf16[256,384,6]{1,2,0:T(8,128)(2,1)S(1)}, u32[]{:S(2)}, u32[]{:S(2)}) %all-to-all-start) | async-done | bytes 1179680 | tf_op jit(solution)/shard_map/all_to_all | solution.py:11
  70.8 1.3 reshape.70
  72.0 3.1 multiply_convert_fusion
  75.1 656.1 %all-gather.3.cloned.1.call-done = bf16[256,6,384]{2,1,0:T(8,128)(2,1)} async-done(((bf16[1,6,384]{2,1,0:T(8,128)(2,1)}), bf16[256,6,384]{2,1,0:T(8,128)(2,1)}) %all-gather.3.cloned.1.call-update) | async-done | bytes 1179664 | tf_op jit(solution)/shard_map/all_gather | solution.py:62
  731.3 3.3 reshape.76
  734.6 2.6 fusion.60
  737.1 2.0 fusion.66
  739.4 0.9 convert_reduce_fusion
  740.3 2.0 fusion.65
  743.0 0.9 multiply_reduce_fusion.1
  743.9 0.7 multiply_reduce_fusion.19
  745.8 4.4 concatenate.19
  750.4 1.9 collective-permute-start.5
  752.4 5.1 collective-permute-start.4
  758.0 0.9 collective-permute-done.4
  758.9 1.9 collective-permute-start.7
  760.9 3.5 collective-permute-start.6
  764.4 74.1 %psum.15 = f32[1536]{0:T(1024)} all-reduce(f32[1536]{0:T(1024)S(1)} %get-tuple-element.129), channel_id=1, replica_groups=mesh['row'=32,'col'=8] {'row','col'}, use_global_device_ids=true, to_apply=%region_61.0 | all-reduce | flops 1536 | bytes 12288 | tf_op jit(solution)/shard_map/psum | solution.py:133
  838.8 3.5 fusion.9
  842.3 176.7 %all-reduce.5.cloned.1.call-done = (f32[384,1536]{0,1:T(8,128)}, f32[1536,384]{1,0:T(8,128)}, f32[53,384]{1,0:T(8,128)}) async-done(((f32[384,1536]{0,1:T(8,128)}, f32[1536,384]{1,0:T(8,128)}, f32[53,384]{1,0:T(8,128)}), (f32[384,1536]{0,1:T(8,128)}, f32[1536,384]{1,0:T(8,128)}, f32[53,384]{1,0:T(8,128)})) %all-reduce.5.cloned.1.call-update) | async-done | bytes 4800016
  1019.0 1.3 constant_dynamic-slice_fusion.1
  1020.3 1.3 constant_dynamic-slice_fusion
  1021.7 1.5 copy.26
  (176 shorter events, 4.7 us)
Async XLA Ops:
  8.1 25.0 %collective-permute-start = (bf16[3,32,384]{2,1,0:T(8,128)(2,1)S(1)}, bf16[3,32,384]{2,1,0:T(8,128)(2,1)S(1)}, u32[]{:S(2)}, u32[]{:S(2)}) collective-permute-start(bf16[3,32,384]{2,1,0:T(8,128)(2,1)S(1)} %get-tuple-element.125), channel_id=1, source_target_pairs={{0,8},{8,16},{16,24},{24,32},{32,40},{40,48},{48,56},{56,64},{64,7... | collective-permute-start | bytes 221192 | tf_op jit(solution)/shard_map/ppermute | solution.py:23
  13.5 19.7 %collective-permute-start.1 = (bf16[3,32,384]{2,1,0:T(8,128)(2,1)S(1)}, bf16[3,32,384]{2,1,0:T(8,128)(2,1)S(1)}, u32[]{:S(2)}, u32[]{:S(2)}) collective-permute-start(bf16[3,32,384]{2,1,0:T(8,128)(2,1)S(1)} %get-tuple-element.124), channel_id=1, source_target_pairs={{8,0},{16,8},{24,16},{32,24},{40,32},{48,40},{56,48},{64,56},{72,6... | collective-permute-start | bytes 221192 | tf_op jit(solution)/shard_map/ppermute | solution.py:24
  17.4 15.5 %copy-start.44 = (f32[384]{0:T(512)S(1)}, f32[384]{0:T(512)}, u32[]{:S(2)}) copy-start(f32[384]{0:T(512)} %param.18) | copy-start | bytes 4612
  17.4 15.8 %copy-start.4 = (bf16[8,32,384]{2,1,0:T(8,128)(2,1)S(1)}, bf16[8,32,384]{2,1,0:T(8,128)(2,1)}, u32[]{:S(2)}) copy-start(bf16[8,32,384]{2,1,0:T(8,128)(2,1)} %param.10) | copy-start | bytes 589828
  17.4 53.4 %all-to-all-start = ((bf16[256,384,6]{1,2,0:T(8,128)(2,1)}), bf16[256,384,6]{1,2,0:T(8,128)(2,1)S(1)}, u32[]{:S(2)}, u32[]{:S(2)}) async-start(bf16[256,384,6]{1,2,0:T(8,128)(2,1)} %stack.100), calls=%async_computation | async-start | bytes 3145728 | tf_op jit(solution)/shard_map/all_to_all | solution.py:11
  32.0 699.3 %all-gather.3.cloned.1.call-start = ((), (), s32[]{:S(2)}) async-start(), calls=%async_computation.1 | async-start | bytes 1579008 | tf_op jit(solution)/shard_map/all_gather | solution.py:62
  32.7 986.2 %all-reduce.5.cloned.1.call-start = ((), (), s32[]{:S(2)}) async-start(), calls=%async_computation.2 | async-start | bytes 9609216
  33.3 6.0 collective-permute-start.3
  36.4 6.1 collective-permute-start.2
  75.1 659.4 %copy-start.45 = (f32[384]{0:T(512)S(1)}, f32[384]{0:T(512)}, u32[]{:S(2)}) copy-start(f32[384]{0:T(512)} %param.18) | copy-start | bytes 4612
  75.1 659.4 %copy-start.46 = (f32[384]{0:T(512)S(1)}, f32[384]{0:T(512)}, u32[]{:S(2)}) copy-start(f32[384]{0:T(512)} %param.17) | copy-start | bytes 4612
  750.2 88.4 %copy-start.7 = (f32[384]{0:T(512)S(1)}, f32[384]{0:T(512)}, u32[]{:S(2)}) copy-start(f32[384]{0:T(512)} %copy-done.6) | copy-start | bytes 4612
  750.2 88.4 %copy-start.9 = (f32[384]{0:T(512)S(1)}, f32[384]{0:T(512)}, u32[]{:S(2)}) copy-start(f32[384]{0:T(512)} %copy-done.8) | copy-start | bytes 4612
  750.2 88.4 %copy-start.11 = (f32[384]{0:T(512)S(1)}, f32[384]{0:T(512)}, u32[]{:S(2)}) copy-start(f32[384]{0:T(512)} %copy-done.10) | copy-start | bytes 4612
  750.3 88.4 %copy-start.13 = (f32[384]{0:T(512)S(1)}, f32[384]{0:T(512)}, u32[]{:S(2)}) copy-start(f32[384]{0:T(512)} %copy-done.12) | copy-start | bytes 4612
  750.3 88.4 %copy-start.15 = (f32[384]{0:T(512)S(1)}, f32[384]{0:T(512)}, u32[]{:S(2)}) copy-start(f32[384]{0:T(512)} %copy-done.14) | copy-start | bytes 4612
  750.3 88.4 %copy-start.17 = (f32[384]{0:T(512)S(1)}, f32[384]{0:T(512)}, u32[]{:S(2)}) copy-start(f32[384]{0:T(512)} %copy-done.16) | copy-start | bytes 4612
  750.3 88.4 %copy-start.19 = (f32[384]{0:T(512)S(1)}, f32[384]{0:T(512)}, u32[]{:S(2)}) copy-start(f32[384]{0:T(512)} %copy-done.18) | copy-start | bytes 4612
  750.3 88.4 %copy-start.21 = (f32[384]{0:T(512)S(1)}, f32[384]{0:T(512)}, u32[]{:S(2)}) copy-start(f32[384]{0:T(512)} %copy-done.20) | copy-start | bytes 4612
  750.3 88.4 %copy-start.23 = (f32[384]{0:T(512)S(1)}, f32[384]{0:T(512)}, u32[]{:S(2)}) copy-start(f32[384]{0:T(512)} %copy-done.22) | copy-start | bytes 4612
  750.3 88.4 %copy-start.25 = (f32[384]{0:T(512)S(1)}, f32[384]{0:T(512)}, u32[]{:S(2)}) copy-start(f32[384]{0:T(512)} %copy-done.24) | copy-start | bytes 4612
  750.3 88.4 %copy-start.27 = (f32[384]{0:T(512)S(1)}, f32[384]{0:T(512)}, u32[]{:S(2)}) copy-start(f32[384]{0:T(512)} %copy-done.26) | copy-start | bytes 4612
  750.3 88.4 %copy-start.29 = (f32[384]{0:T(512)S(1)}, f32[384]{0:T(512)}, u32[]{:S(2)}) copy-start(f32[384]{0:T(512)} %copy-done.28) | copy-start | bytes 4612
  750.3 88.4 %copy-start.31 = (f32[384]{0:T(512)S(1)}, f32[384]{0:T(512)}, u32[]{:S(2)}) copy-start(f32[384]{0:T(512)} %copy-done.30) | copy-start | bytes 4612
  750.4 88.4 %copy-start.33 = (f32[384]{0:T(512)S(1)}, f32[384]{0:T(512)}, u32[]{:S(2)}) copy-start(f32[384]{0:T(512)} %copy-done.32) | copy-start | bytes 4612
  750.4 88.4 %copy-start.35 = (f32[384]{0:T(512)S(1)}, f32[384]{0:T(512)}, u32[]{:S(2)}) copy-start(f32[384]{0:T(512)} %copy-done.34) | copy-start | bytes 4612
  750.4 88.4 %copy-start.37 = (f32[384]{0:T(512)S(1)}, f32[384]{0:T(512)}, u32[]{:S(2)}) copy-start(f32[384]{0:T(512)} %copy-done.36) | copy-start | bytes 4612
  750.4 88.4 %copy-start.39 = (f32[384]{0:T(512)S(1)}, f32[384]{0:T(512)}, u32[]{:S(2)}) copy-start(f32[384]{0:T(512)} %copy-done.38) | copy-start | bytes 4612
  750.4 7.5 collective-permute-start.5
  752.4 6.5 collective-permute-start.4
  758.9 79.6 %collective-permute-start.7 = (bf16[14,3,384]{2,1,0:T(4,128)(2,1)S(1)}, bf16[14,3,384]{2,1,0:T(4,128)(2,1)S(1)}, u32[]{:S(2)}, u32[]{:S(2)}) collective-permute-start(bf16[14,3,384]{2,1,0:T(4,128)(2,1)S(1)} %get-tuple-element.118), channel_id=1, source_target_pairs={{1,0},{2,1},{3,2},{4,3},{5,4},{6,5},{7,6},{9,8},{10,9},{11,10},{12... | collective-permute-start | bytes 96776 | tf_op jit(solution)/shard_map/ppermute | solution.py:24
  760.9 77.6 %collective-permute-start.6 = (bf16[14,3,384]{2,1,0:T(4,128)(2,1)S(1)}, bf16[14,3,384]{2,1,0:T(4,128)(2,1)S(1)}, u32[]{:S(2)}, u32[]{:S(2)}) collective-permute-start(bf16[14,3,384]{2,1,0:T(4,128)(2,1)S(1)} %get-tuple-element.117), channel_id=1, source_target_pairs={{0,1},{1,2},{2,3},{3,4},{4,5},{5,6},{6,7},{8,9},{9,10},{10,11},{11... | collective-permute-start | bytes 96776 | tf_op jit(solution)/shard_map/ppermute | solution.py:23
  (26 other events, 204.1 us)
Sparse Core Ops, SparseCore 0:
  34.7 696.4 all-gather.2
  750.3 268.5 all-reduce.4
